TPU v7x, 32 devices: a whole 2x2x4 slice. The times are simulated.
32 devices in a mesh: prow: 4 (over y, x), pcol: 8 (over z, core).
Axes of the slice: x: 2, y: 2, z: 4, core: 2. Of those that a mesh axis runs over, the one named last changes fastest.
Arguments:
- ancestor: float32 [12288, 12288], P('prow', 'pcol'), may hold values from -448 to 15360, as said below
- factor: bfloat16 [2, 12288, 256], P(None, 'prow'), may hold values from -0.0009765625 to 0.0009765625
- inverse_diag: bfloat16 [2, 256, 256], replicated, may hold values from -6 to 6
- block_mask: int32 [2, 48], replicated, may hold values 0 or 1
Outputs:
- column_block: float32 [2, 12288, 256], P(None, ('prow', 'pcol'))
- diagonal: float32 [2, 256, 256], replicated
Inputs may be any that keep to these rules, and one draw needn't show every extreme that they name: `ancestor`: symmetric.
All inputs are finite; a program needn't handle non-finite values.
Results may differ from a plain program's by a relative error of at most 0.0003.
Values may be sent and summed in bfloat16 or wider, within the bound.
A program may use at most 64 MiB of HBM per device.

v0:
```python
import jax
import jax.numpy as jnp
from jax import lax
from jax.sharding import PartitionSpec as P

WIDTH = 256


def broadcast(shard, axis, root):
    mine = lax.axis_index(axis) == root
    return lax.psum(jnp.where(mine, shard, jnp.zeros_like(shard)), axis)


def multiply(ancestor, received, col_mask, own_mask):
    weighted = received.astype(jnp.float32) * col_mask[:, :, None]
    product = jnp.einsum(
        "ij,kjw->kiw",
        ancestor,
        weighted,
        precision=lax.Precision.HIGHEST,
        preferred_element_type=jnp.float32,
    )
    return -own_mask[:, :, None] * product


def reduced_term(own_rows, column_block, column):
    slab = column_block.shape[1]
    own_slab = lax.dynamic_slice_in_dim(own_rows, column * slab, slab, 1)
    return jnp.einsum(
        "kiw,kiv->kwv",
        own_slab,
        column_block,
        precision=lax.Precision.HIGHEST,
        preferred_element_type=jnp.float32,
    )


def shards(ancestor, factor, inverse_diag, block_mask):
    rows_here = ancestor.shape[0]
    cols_here = ancestor.shape[1]
    n_rows = lax.axis_size("prow")
    n_cols = lax.axis_size("pcol")
    per_row = n_cols // n_rows
    column = lax.axis_index("pcol")
    grid_row = lax.axis_index("prow")
    root_row = column // per_row
    offset = column % per_row * cols_here
    row_mask = jnp.repeat(block_mask, WIDTH, axis=1).astype(jnp.float32)
    own_mask = lax.dynamic_slice_in_dim(row_mask, grid_row * rows_here, rows_here, 1)
    col_mask = lax.dynamic_slice_in_dim(row_mask, column * cols_here, cols_here, 1)
    own_rows = factor.astype(jnp.float32) * own_mask[:, :, None]
    col_part = lax.dynamic_slice_in_dim(factor, offset, cols_here, 1)
    pieces = []
    blocks = []
    for supernode in range(factor.shape[0]):
        received = broadcast(col_part[supernode : supernode + 1], "prow", root_row)
        negated_one = multiply(
            ancestor,
            received,
            col_mask[supernode : supernode + 1],
            own_mask[supernode : supernode + 1],
        )
        blocks.append(lax.psum_scatter(negated_one, "pcol", scatter_dimension=1, tiled=True))
        pieces.append(negated_one)
    column_block = jnp.concatenate(blocks, 0)
    term = reduced_term(own_rows, column_block, column)
    total = lax.psum(term, ("prow", "pcol"))
    diagonal = inverse_diag.astype(jnp.float32) - total
    return (column_block, diagonal)


def solution(mesh):
    return jax.shard_map(
        shards,
        mesh=mesh,
        in_specs=(P("prow", "pcol"), P(None, "prow", None), P(), P()),
        out_specs=(P(None, ("prow", "pcol"), None), P()),
        check_vma=False,
    )
```

profile of v0, /device:TPU:0, one launch (start us, length us, event | category | flops | bytes accessed | tf_op | source)
XLA Modules:
  0.0 335.2 jit_solution(11929056268012232022)
XLA Ops:
  7.2 0.0 all-reduce.6.cloned.1.call-start
  7.2 2.8 dynamic-slice_select_fusion
  10.1 0.0 reduce-scatter.3.cloned.1.call-start
  10.2 0.1 broadcast_bitcast_fusion
  10.2 0.1 copy.11
  10.3 0.1 dynamic-slice_reduce_fusion
  10.4 0.1 dynamic-slice_negate_fusion
  10.5 64.6 %all-reduce.6.cloned.1.call-done = (bf16[1,1536,256]{2,1,0:T(8,128)(2,1)}, bf16[1,1536,256]{2,1,0:T(8,128)(2,1)}) async-done(((bf16[1,1536,256]{2,1,0:T(8,128)(2,1)}, bf16[1,1536,256]{2,1,0:T(8,128)(2,1)}), (bf16[1,1536,256]{2,1,0:T(8,128)(2,1)}, bf16[1,1536,256]{2,1,0:T(8,128)(2,1)})) %all-reduce.6.cloned.1.call-update) | async-done | bytes 1572880 | tf_op jit(solution)/shard_map/psum | solution.py:11
  75.2 35.3 %fusion.3 = f32[1,3072,256]{1,2,0:T(8,128)} fusion(f32[3072,1536]{1,0:T(8,128)} %param.4, bf16[1,1536,256]{2,1,0:T(8,128)(2,1)} %get-tuple-element.6, f32[3072]{0:T(1024)S(1)} %bitcast.34, f32[1536]{0:T(1024)S(1)} %get-tuple-element.5), kind=kOutput, calls=%fused_computation.5 | convolution fusion | flops 14497087488 | bytes 22824960 | tf_op jit(solution)/shard_map/ij,kjw->kiw/dot_general | solution.py:16
  110.4 0.0 reduce-scatter.3.cloned.1.call-update
  110.4 0.2 reduce-scatter.5.cloned.1.call-start
  110.7 0.9 copy-done
  111.5 35.1 %fusion.1 = f32[1,3072,256]{1,2,0:T(8,128)} fusion(f32[3072,1536]{1,0:T(8,128)} %param.4, bf16[1,1536,256]{2,1,0:T(8,128)(2,1)S(1)} %copy-done, f32[3072]{0:T(1024)S(1)} %bitcast.33, f32[1536]{0:T(1024)S(1)} %get-tuple-element.4), kind=kOutput, calls=%fused_computation.2 | convolution fusion | flops 14497087488 | bytes 22824960 | tf_op jit(solution)/shard_map/ij,kjw->kiw/dot_general | solution.py:16
  146.7 0.0 all-reduce.4.cloned.1.call-start
  146.7 1.0 constant_dynamic-slice_fusion.1
  147.8 0.2 copy.10
  148.0 2.9 reduce-scatter.3.cloned.1.call-done
  151.0 1.0 constant_dynamic-update-slice_fusion.1
  152.0 40.8 %reduce-scatter.5.cloned.1.call-done = f32[1,384,256]{1,2,0:T(8,128)} async-done(((f32[1,3072,256]{1,2,0:T(8,128)}), f32[1,384,256]{1,2,0:T(8,128)}) %reduce-scatter.5.cloned.1.call-update) | async-done | bytes 393232 | tf_op jit(solution)/shard_map/reduce_scatter | solution.py:63
  192.8 1.0 constant_dynamic-update-slice_fusion
  193.9 1.9 fusion.10
  195.8 1.1 copy.8
  197.0 129.8 %all-reduce.4.cloned.1.call-done = f32[2,256,256]{2,1,0:T(8,128)} async-done(((f32[2,256,256]{2,1,0:T(8,128)}), f32[2,256,256]{2,1,0:T(8,128)}) %all-reduce.4.cloned.1.call-update) | async-done | bytes 524304 | tf_op jit(solution)/shard_map/psum | solution.py:67
  326.8 1.9 convert_subtract_fusion
  (11 shorter events, 0.1 us)
Async XLA Ops:
  7.2 3.0 copy-start.2
  7.2 68.0 %all-reduce.6.cloned.1.call-start = ((), (), s32[]{:S(2)}) async-start(), calls=%async_computation.5 | async-start | bytes 3145728 | tf_op jit(solution)/shard_map/psum | solution.py:11
  10.1 140.9 %reduce-scatter.3.cloned.1.call-start = ((), (), s32[]{:S(2)}) async-start(), calls=%async_computation.2 | async-start | bytes 3538944 | tf_op jit(solution)/shard_map/reduce_scatter | solution.py:63
  110.4 1.1 copy-start
  110.4 82.4 %reduce-scatter.5.cloned.1.call-start = ((), (), s32[]{:S(2)}) async-start(), calls=%async_computation.3 | async-start | bytes 3538944 | tf_op jit(solution)/shard_map/reduce_scatter | solution.py:63
  146.7 180.1 %all-reduce.4.cloned.1.call-start = ((), (), s32[]{:S(2)}) async-start(), calls=%async_computation.4 | async-start | bytes 1048576 | tf_op jit(solution)/shard_map/psum | solution.py:67
  147.8 179.0 %copy-start.1 = (bf16[2,256,256]{2,1,0:T(8,128)(2,1)S(1)}, bf16[2,256,256]{2,1,0:T(8,128)(2,1)}, u32[]{:S(2)}) copy-start(bf16[2,256,256]{2,1,0:T(8,128)(2,1)} %param.6) | copy-start | bytes 786436
Sparse Core Ops, SparseCore 0:
  11.7 63.4 all-reduce.5
  110.6 40.3 reduce-scatter.2
  153.3 39.5 reduce-scatter.4
  198.5 128.1 all-reduce.3
where the time goes:
time: 336 us; the launch traced here: 335 us
  waiting for transfers between devices  238 us (71%)
  matrix products  72.3 us (22%)
  between operations  13.9 us (4%)
  local copies, waits for them, and re-layouts  5.6 us (2%)
  other arithmetic  4.8 us (1%)
    psum x1, waiting for transfers between devices, shards(): total = lax.psum(term, ('prow', 'pcol'))  130 us
    dot_general x2, matrix products, multiply(): jnp.einsum('ij,kjw->kiw', ancestor, weighted, precision=lax.Precision.HIG...  70.4 us
    psum x1, waiting for transfers between devices, broadcast(): return lax.psum(jnp.where(mine, shard, jnp.zeros_like(shard)), axis)  64.6 us
    reduce_scatter x2, waiting for transfers between devices, shards(): lax.psum_scatter(negated_one, 'pcol', scatter_dimension=1, tiled=True)  43.8 us
  transfers between devices with their start and end apart: 4, of which 4 were waited for; matrix products, arithmetic and copies ran while one was open for 12% of the time, Pallas kernels for 0%

commit v1 on v0

v1 whole, which is shorter than its diff:
```python
import jax
import jax.numpy as jnp
from jax import lax
from jax.sharding import PartitionSpec as P

WIDTH = 256


def split(x):
    high = lax.reduce_precision(x, 8, 7)
    low = x - high
    return high.astype(jnp.bfloat16), low.astype(jnp.bfloat16)


def dot(a, b):
    return jnp.dot(a, b, preferred_element_type=jnp.float32)


def shards(ancestor, factor, inverse_diag, block_mask):
    rows_here = ancestor.shape[0]
    count, _, width = factor.shape
    n_rows = lax.axis_size("prow")
    n_cols = lax.axis_size("pcol")
    column = lax.axis_index("pcol")
    grid_row = lax.axis_index("prow")
    slab = rows_here // n_cols
    row_mask = jnp.repeat(block_mask, WIDTH, axis=1).astype(jnp.float32)
    own_mask = lax.dynamic_slice_in_dim(row_mask, grid_row * rows_here, rows_here, 1)
    masked = factor * own_mask[:, :, None].astype(factor.dtype)
    turned = masked.transpose(0, 2, 1).reshape(count * width, rows_here)
    high, low = split(ancestor)
    partial = dot(turned, high) + dot(turned, low)
    summed = lax.psum_scatter(partial, "prow", scatter_dimension=1, tiled=True)
    pairs = [(r * n_cols + c, c * n_rows + r) for r in range(n_rows) for c in range(n_cols)]
    placed = lax.ppermute(summed, ("prow", "pcol"), pairs)
    slab_mask = lax.dynamic_slice_in_dim(own_mask, column * slab, slab, 1)
    placed = placed.reshape(count, width, slab)
    column_block = -slab_mask[:, :, None] * placed.transpose(0, 2, 1)
    own_slab = lax.dynamic_slice_in_dim(masked, column * slab, slab, 1)
    high, low = split(column_block)
    term = jnp.stack([dot(own_slab[k].T, high[k]) + dot(own_slab[k].T, low[k]) for k in range(count)])
    total = lax.psum(term, ("prow", "pcol"))
    diagonal = inverse_diag.astype(jnp.float32) - total
    return (column_block, diagonal)


def solution(mesh):
    return jax.shard_map(
        shards,
        mesh=mesh,
        in_specs=(P("prow", "pcol"), P(None, "prow", None), P(), P()),
        out_specs=(P(None, ("prow", "pcol"), None), P()),
        check_vma=False,
    )
```

time: 336 us -> 255 us (0.76)
  matrix products: 72.3 us -> 26.3 us
  waiting for transfers between devices: 238 us -> 205 us
    psum x1 -> x0, waiting for transfers between devices: 64.6 us -> none  [broadcast(): return lax.psum(jnp.where(mine, shard, jnp.zeros_like(shard)), axis)]
    dot_general x3 -> x6, matrix products: 72.3 us -> 26.3 us  [dot(): return jnp.dot(a, b, preferred_element_type=jnp.float32)]
    psum x1, waiting for transfers between devices: 130 us -> 158 us  [shards(): total = lax.psum(term, ('prow', 'pcol'))]
    reduce_scatter x2 -> x1, waiting for transfers between devices: 43.8 us -> 46.7 us  [shards(): summed = lax.psum_scatter(partial, 'prow', scatter_dimension=1, tiled=True)]
  transfers between devices with their start and end apart: 4 -> 3, of which waited for: 4 -> 2; matrix products, arithmetic and copies ran while one was open for 12% -> 0% of each run, Pallas kernels for 0% -> 0%
where the time goes in v1:
time: 255 us; the launch traced here: 254 us
  waiting for transfers between devices  205 us (80%)
  matrix products  26.3 us (10%)
  between operations  14.2 us (6%)
  other arithmetic  3.91 us (2%)
  local copies, waits for them, and re-layouts  3.65 us (1%)
    psum x1, waiting for transfers between devices, shards(): total = lax.psum(term, ('prow', 'pcol'))  158 us
    reduce_scatter x1, waiting for transfers between devices, shards(): summed = lax.psum_scatter(partial, 'prow', scatter_dimension=1, tiled=True)  46.7 us
    dot_general x6, matrix products, dot(): return jnp.dot(a, b, preferred_element_type=jnp.float32)  26.3 us
  transfers between devices with their start and end apart: 3, of which 2 were waited for; matrix products, arithmetic and copies ran while one was open for 0% of the time, Pallas kernels for 0%

profile of v1, /device:TPU:0, one launch (start us, length us, event | category | flops | bytes accessed | tf_op | source)
XLA Modules:
  0.0 254.4 jit_solution(12898401769275026924)
XLA Ops:
  7.2 0.0 reduce-scatter.2.cloned.1.call-start
  7.2 0.7 convert_element_type.26
  7.9 0.1 broadcast_bitcast_fusion
  8.0 0.1 copy.9
  8.1 3.2 %copy.7 = bf16[2,3072,256]{1,2,0:T(8,128)(2,1)S(1)} copy(bf16[2,3072,256]{2,1,0:T(8,128)(2,1)} %param.5) | data formatting | bytes 6291456 | tf_op args[1]
  11.3 0.2 broadcast_multiply_fusion
  11.5 10.2 %fusion.1 = f32[512,1536]{1,0:T(8,128)S(1)} fusion(bf16[512,3072]{1,0:T(8,128)(2,1)S(1)} %bitcast.36, f32[3072,1536]{1,0:T(8,128)} %param.4), kind=kOutput, calls=%fused_computation.3 | convolution fusion | flops 4845993984 | bytes 25165824 | tf_op jit(solution)/shard_map/dot_general | solution.py:16
  21.7 11.2 %fusion.4 = f32[512,1536]{1,0:T(8,128)} fusion(f32[512,1536]{1,0:T(8,128)S(1)} %fusion.1, bf16[512,3072]{1,0:T(8,128)(2,1)S(1)} %bitcast.37, f32[3072,1536]{1,0:T(8,128)} %param.4), kind=kOutput, calls=%fused_computation.5 | convolution fusion | flops 4842061824 | bytes 28311552 | tf_op jit(solution)/shard_map/dot_general | solution.py:16
  33.0 0.0 reduce-scatter.2.cloned.1.call-update
  33.0 0.0 all-reduce.2.cloned.1.call-start
  33.0 46.7 %reduce-scatter.2.cloned.1.call-done = f32[512,384]{1,0:T(8,128)} async-done(((f32[512,1536]{1,0:T(8,128)}), f32[512,384]{1,0:T(8,128)}) %reduce-scatter.2.cloned.1.call-update) | async-done | bytes 786448 | tf_op jit(solution)/shard_map/reduce_scatter | solution.py:33
  79.8 1.8 collective-permute-start
  81.6 0.1 dynamic-slice_negate_fusion
  81.6 0.3 copy.8
  81.9 0.2 fusion.7
  82.1 0.0 copy-start.1
  82.2 1.4 fusion.9
  83.6 1.2 fusion.8
  84.8 1.2 fusion.5
  85.9 1.2 fusion.6
  87.1 0.8 pad_maximum_fusion
  87.9 0.0 all-reduce.2.cloned.1.call-update
  87.9 157.7 %all-reduce.2.cloned.1.call-done = f32[2,256,256]{2,1,0:T(8,128)} async-done(((f32[2,256,256]{2,1,0:T(8,128)}), f32[2,256,256]{2,1,0:T(8,128)}) %all-reduce.2.cloned.1.call-update) | async-done | bytes 524304 | tf_op jit(solution)/shard_map/psum | solution.py:42
  245.7 1.9 convert_subtract_fusion
  (8 shorter events, 0.1 us)
Async XLA Ops:
  7.2 72.6 %reduce-scatter.2.cloned.1.call-start = ((), (), s32[]{:S(2)}) async-start(), calls=%async_computation.1 | async-start | bytes 3932160 | tf_op jit(solution)/shard_map/reduce_scatter | solution.py:33
  11.5 10.2 %copy-start = (bf16[2,3072,256]{1,2,0:T(8,128)(2,1)}, bf16[2,3072,256]{1,2,0:T(8,128)(2,1)S(1)}, u32[]{:S(2)}) copy-start(bf16[2,3072,256]{1,2,0:T(8,128)(2,1)S(1)} %broadcast_multiply_fusion) | copy-start | bytes 9437188
  33.0 212.7 %all-reduce.2.cloned.1.call-start = ((), (), s32[]{:S(2)}) async-start(), calls=%async_computation.2 | async-start | bytes 1048576 | tf_op jit(solution)/shard_map/psum | solution.py:42
  79.8 1.9 collective-permute-start
  82.1 165.5 %copy-start.1 = (f32[2,384,256]{2,1,0:T(8,128)}, f32[2,384,256]{2,1,0:T(8,128)S(1)}, u32[]{:S(2)}) copy-start(f32[2,384,256]{2,1,0:T(8,128)S(1)} %get-tuple-element.3) | copy-start | bytes 2359300
  82.1 163.6 %copy-start.2 = (bf16[2,256,256]{2,1,0:T(8,128)(2,1)S(1)}, bf16[2,256,256]{2,1,0:T(8,128)(2,1)}, u32[]{:S(2)}) copy-start(bf16[2,256,256]{2,1,0:T(8,128)(2,1)} %param.6) | copy-start | bytes 786436
Sparse Core Ops, SparseCore 0:
  33.1 46.6 reduce-scatter.1
  88.1 157.5 all-reduce.1

commit v2 on v1

--- a/solution.py
+++ b/solution.py
@@ -1,6 +1,8 @@
 import jax
 import jax.numpy as jnp
 from jax import lax
+from jax.experimental import pallas as pl
+from jax.experimental.pallas import tpu as pltpu
 from jax.sharding import PartitionSpec as P
 
 WIDTH = 256
@@ -14,6 +16,113 @@
 
 def dot(a, b):
     return jnp.dot(a, b, preferred_element_type=jnp.float32)
+
+
+MESH = pl.DeviceIdType.MESH
+
+
+def levels():
+    n_rows = lax.axis_size("prow")
+    n_deep = lax.axis_size("pcol") // 2
+    row = lax.axis_index("prow")
+    column = lax.axis_index("pcol")
+    deep, core = lax.div(column, 2), lax.rem(column, 2)
+    return (
+        (2, core, lambda p: (row, deep * 2 + p)),
+        (n_rows, row, lambda p: (p, column)),
+        (n_deep, deep, lambda p: (row, p * 2 + core)),
+    )
+
+
+def greet(peers):
+    barrier = pltpu.get_barrier_semaphore()
+    for peer in peers:
+        pl.semaphore_signal(barrier, inc=1, device_id=peer, device_id_type=MESH)
+    pl.semaphore_wait(barrier, len(peers))
+
+
+def part(ref, start, size):
+    return ref.at[pl.ds(pl.multiple_of(start, 8), size)]
+
+
+def sum_everywhere(term, acc, landed, gathered, sems):
+    height = term.shape[0]
+    start = 0
+    size = height
+    source = term
+    sent = []
+    starts = []
+    number = 0
+    slot = 0
+    for n, mine, device in levels():
+        size = size // n
+        copies = []
+        for d in range(1, n):
+            peer = lax.rem(mine + d, n)
+            copy = pltpu.make_async_remote_copy(
+                part(source, start + peer * size, size),
+                landed.at[pl.ds(slot + (d - 1) * size, size)],
+                sems.at[0, number],
+                sems.at[1, number],
+                device_id=device(peer),
+                device_id_type=MESH,
+            )
+            copy.start()
+            copies.append(copy)
+            number += 1
+        start = start + mine * size
+        starts.append((start, size))
+        total = part(source, start, size)[...]
+        for d in range(1, n):
+            copies[d - 1].wait_recv()
+            total = total + landed[pl.ds(slot + (d - 1) * size, size)]
+        slot += (n - 1) * size
+        part(acc, start, size)[...] = total
+        source = acc
+        sent += copies
+    part(gathered, start, size)[...] = total
+    for (n, mine, device), (start, size) in reversed(list(zip(levels(), starts))):
+        copies = []
+        for d in range(1, n):
+            peer = lax.rem(mine + d, n)
+            copy = pltpu.make_async_remote_copy(
+                part(gathered, start, size),
+                part(gathered, start, size),
+                sems.at[0, number],
+                sems.at[1, number],
+                device_id=device(peer),
+                device_id_type=MESH,
+            )
+            copy.start()
+            copies.append(copy)
+            number += 1
+        for copy in copies:
+            copy.wait_recv()
+        sent += copies
+    for copy in sent:
+        copy.wait_send()
+
+
+def diagonal_kernel(term, inverse, out, acc, landed, gathered, sems):
+    greet([device(lax.rem(mine + d, n)) for n, mine, device in levels() for d in range(1, n)])
+    sum_everywhere(term, acc, landed, gathered, sems)
+    out[...] = inverse[...].astype(jnp.float32) - gathered[...]
+
+
+def finish(term, inverse):
+    height, width = term.shape
+    sizes = [2, lax.axis_size("prow"), lax.axis_size("pcol") // 2]
+    copies = sum(n - 1 for n in sizes) * 2
+    block = pltpu.VMEM((height, width), jnp.float32)
+    vmem = pl.BlockSpec(memory_space=pltpu.VMEM)
+    return pl.pallas_call(
+        diagonal_kernel,
+        out_shape=jax.ShapeDtypeStruct((height, width), jnp.float32),
+        in_specs=[vmem, vmem],
+        out_specs=vmem,
+        scratch_shapes=[block, block, block, pltpu.SemaphoreType.DMA((2, copies))],
+        compiler_params=pltpu.CompilerParams(collective_id=0, has_side_effects=True),
+    )(term, inverse)
 
 
 def shards(ancestor, factor, inverse_diag, block_mask):
@@ -39,9 +148,13 @@
     own_slab = lax.dynamic_slice_in_dim(masked, column * slab, slab, 1)
     high, low = split(column_block)
     term = jnp.stack([dot(own_slab[k].T, high[k]) + dot(own_slab[k].T, low[k]) for k in range(count)])
-    total = lax.psum(term, ("prow", "pcol"))
-    diagonal = inverse_diag.astype(jnp.float32) - total
-    return (column_block, diagonal)
+    devices = n_rows * n_cols
+    if n_cols % 2 or (count * width) % (8 * devices):
+        total = lax.psum(term, ("prow", "pcol"))
+        return (column_block, inverse_diag.astype(jnp.float32) - total)
+    flat = (count * width, width)
+    diagonal = finish(term.reshape(flat), inverse_diag.reshape(flat))
+    return (column_block, diagonal.reshape(inverse_diag.shape))
 
 
 def solution(mesh):

time: 255 us -> 151 us (0.59)
  waiting for transfers between devices: 205 us -> 46.8 us
  Pallas kernels: 0 us -> 53.9 us
    psum x1 -> x0, waiting for transfers between devices: 158 us -> none  [shards(): total = lax.psum(term, ('prow', 'pcol'))]
    pallas_call x0 -> x1, Pallas kernels: none -> 53.9 us  [finish(): pl.pallas_call(diagonal_kernel, out_shape=jax.ShapeDtypeStruct((height, w...]
    unnamed x9 -> x8, local copies, waits for them, and re-layouts: 3.36 us -> 5.23 us
  transfers between devices with their start and end apart: 3 -> 2, of which waited for: 2 -> 1; matrix products, arithmetic and copies ran while one was open for 0% -> 0% of each run, Pallas kernels for 0% -> 0%
where the time goes in v2:
time: 151 us; the launch traced here: 150 us
  Pallas kernels  53.9 us (36%)
  waiting for transfers between devices  46.8 us (31%)
  matrix products  26.3 us (17%)
  between operations  14.2 us (9%)
  local copies, waits for them, and re-layouts  5.51 us (4%)
  other arithmetic  2.02 us (1%)
  starting transfers between devices  1.82 us (1%)
    pallas_call x1, Pallas kernels, finish(): pl.pallas_call(diagonal_kernel, out_shape=jax.ShapeDtypeStruct((height, w...  53.9 us
    reduce_scatter x1, waiting for transfers between devices, shards(): summed = lax.psum_scatter(partial, 'prow', scatter_dimension=1, tiled=True)  46.8 us
    dot_general x6, matrix products, dot(): return jnp.dot(a, b, preferred_element_type=jnp.float32)  26.3 us
    unnamed x8, local copies, waits for them, and re-layouts  5.23 us
  transfers between devices with their start and end apart: 2, of which 1 were waited for; matrix products, arithmetic and copies ran while one was open for 0% of the time, Pallas kernels for 0%

profile of v2, /device:TPU:0, one launch (start us, length us, event | category | flops | bytes accessed | tf_op | source)
XLA Modules:
  0.0 150.5 jit_solution(14883129799090105130)
XLA Ops:
  7.2 0.0 reduce-scatter.2.cloned.1.call-start
  7.2 0.7 convert_element_type.23
  7.9 0.1 broadcast_bitcast_fusion
  8.0 0.1 copy.9
  8.1 3.2 %copy.7 = bf16[2,3072,256]{1,2,0:T(8,128)(2,1)S(1)} copy(bf16[2,3072,256]{2,1,0:T(8,128)(2,1)} %param.5) | data formatting | bytes 6291456 | tf_op args[1]
  11.3 0.2 broadcast_multiply_fusion
  11.5 0.0 copy-start
  11.5 10.2 %fusion.1 = f32[512,1536]{1,0:T(8,128)S(1)} fusion(bf16[512,3072]{1,0:T(8,128)(2,1)S(1)} %bitcast.39, f32[3072,1536]{1,0:T(8,128)} %param.4), kind=kOutput, calls=%fused_computation.3 | convolution fusion | flops 4845993984 | bytes 25165824 | tf_op jit(solution)/shard_map/dot_general | solution.py:18
  21.7 11.2 %fusion.4 = f32[512,1536]{1,0:T(8,128)} fusion(f32[512,1536]{1,0:T(8,128)S(1)} %fusion.1, bf16[512,3072]{1,0:T(8,128)(2,1)S(1)} %bitcast.40, f32[3072,1536]{1,0:T(8,128)} %param.4), kind=kOutput, calls=%fused_computation.5 | convolution fusion | flops 4842061824 | bytes 28311552 | tf_op jit(solution)/shard_map/dot_general | solution.py:18
  33.0 0.0 reduce-scatter.2.cloned.1.call-update
  33.0 46.8 %reduce-scatter.2.cloned.1.call-done = f32[512,384]{1,0:T(8,128)} async-done(((f32[512,1536]{1,0:T(8,128)}), f32[512,384]{1,0:T(8,128)}) %reduce-scatter.2.cloned.1.call-update) | async-done | bytes 786448 | tf_op jit(solution)/shard_map/reduce_scatter | solution.py:142
  79.8 1.8 %collective-permute-start = (f32[512,384]{1,0:T(8,128)}, f32[512,384]{1,0:T(8,128)S(1)}, u32[]{:S(2)}, u32[]{:S(2)}) collective-permute-start(f32[512,384]{1,0:T(8,128)} %reduce-scatter.2.cloned.1.call-done), channel_id=1, source_target_pairs={{0,0},{1,4},{2,8},{3,12},{4,16},{5,20},{6,24},{7,28},{8,1},{9,5},{... | collective-permute-start | bytes 2359304 | tf_op jit(solution)/shard_map/ppermute | solution.py:144
  81.6 0.1 dynamic-slice_negate_fusion
  81.6 0.0 collective-permute-done
  81.6 0.3 copy.8
  81.9 0.2 fusion.7
  82.1 0.0 copy-start.1
  82.2 1.4 fusion.9
  83.5 1.2 fusion.8
  84.7 1.2 fusion.5
  85.9 1.2 fusion.6
  87.0 0.8 pad_maximum_fusion
  87.9 53.9 %shard_map.59 = f32[512,256]{1,0:T(8,128)} custom-call(f32[512,256]{1,0:T(8,128)} %bitcast.41, bf16[512,256]{1,0:T(8,128)(2,1)} %bitcast.44), custom_call_target="tpu_custom_call" | custom-call | tf_op jit(solution)/shard_map/pallas_call | solution.py:118
  141.8 1.9 %copy.11 = f32[2,256,256]{2,1,0:T(8,128)} copy(f32[2,256,256]{2,1,0:T(8,128)} %bitcast.42) | data formatting | bytes 1048576
  (4 shorter events, 0.1 us)
Async XLA Ops:
  7.2 72.6 %reduce-scatter.2.cloned.1.call-start = ((), (), s32[]{:S(2)}) async-start(), calls=%async_computation.1 | async-start | bytes 3932160 | tf_op jit(solution)/shard_map/reduce_scatter | solution.py:142
  11.5 10.2 %copy-start = (bf16[2,3072,256]{1,2,0:T(8,128)(2,1)}, bf16[2,3072,256]{1,2,0:T(8,128)(2,1)S(1)}, u32[]{:S(2)}) copy-start(bf16[2,3072,256]{1,2,0:T(8,128)(2,1)S(1)} %broadcast_multiply_fusion) | copy-start | bytes 9437188
  79.8 1.9 %collective-permute-start = (f32[512,384]{1,0:T(8,128)}, f32[512,384]{1,0:T(8,128)S(1)}, u32[]{:S(2)}, u32[]{:S(2)}) collective-permute-start(f32[512,384]{1,0:T(8,128)} %reduce-scatter.2.cloned.1.call-done), channel_id=1, source_target_pairs={{0,0},{1,4},{2,8},{3,12},{4,16},{5,20},{6,24},{7,28},{8,1},{9,5},{... | collective-permute-start | bytes 2359304 | tf_op jit(solution)/shard_map/ppermute | solution.py:144
  82.1 59.7 %copy-start.1 = (f32[2,384,256]{2,1,0:T(8,128)}, f32[2,384,256]{2,1,0:T(8,128)S(1)}, u32[]{:S(2)}) copy-start(f32[2,384,256]{2,1,0:T(8,128)S(1)} %get-tuple-element.6) | copy-start | bytes 2359300
Sparse Core Ops, SparseCore 0:
  33.1 46.6 reduce-scatter.1

commit v3 on v2

--- a/solution.py
+++ b/solution.py
@@ -125,6 +125,179 @@
     )(term, inverse)
 
 
+LANES = 128
+
+
+def remote(source, target, sems, piece, number, device):
+    return pltpu.make_async_remote_copy(
+        source,
+        target,
+        sems.at[0, piece, number],
+        sems.at[1, piece, number],
+        device_id=device,
+        device_id_type=MESH,
+    )
+
+
+def product_kernel(turned, ancestor, out, tiles, parts, first, second, sums, ended, landing, loads, sems):
+    n_rows = lax.axis_size("prow")
+    n_cols = lax.axis_size("pcol")
+    row = lax.axis_index("prow")
+    column = lax.axis_index("pcol")
+    slab = out.shape[1]
+    pieces = slab // LANES
+    half = out.shape[0] // 2
+    flip_x = row + 1 - 2 * lax.rem(row, 2)
+    flip_y = lax.rem(row + 2, 4)
+    flip_both = 3 - row
+    x_peer, y_peer = (flip_x, column), (flip_y, column)
+    place = column * n_rows + row
+    target = (lax.div(place, n_cols), lax.rem(place, n_cols))
+    here = row * n_cols + column
+    origin = (lax.rem(here, n_rows), lax.div(here, n_rows))
+    order = (flip_both, flip_x, flip_y, row)
+    buffers = tiles.shape[0]
+    upper, lower = pl.ds(0, half), pl.ds(half, half)
+
+    def load(t):
+        start = pl.multiple_of(order[t % 4] * slab + (t // 4) * LANES, LANES)
+        return pltpu.make_async_copy(ancestor.at[:, pl.ds(start, LANES)], tiles.at[t % buffers], loads.at[t])
+
+    for t in range(buffers):
+        load(t).start()
+
+    barrier = pltpu.get_barrier_semaphore()
+    pl.semaphore_signal(barrier, inc=1, device_id=x_peer, device_id_type=MESH)
+    pl.semaphore_signal(barrier, inc=1, device_id=y_peer, device_id_type=MESH)
+
+    @pl.when(place != here)
+    def _():
+        pl.semaphore_signal(barrier, inc=1, device_id=origin, device_id_type=MESH)
+        pl.semaphore_wait(barrier, 3)
+
+    @pl.when(place == here)
+    def _():
+        pl.semaphore_wait(barrier, 2)
+
+    def early(j):
+        return (
+            remote(parts.at[4 * j, upper], first.at[j, 0], sems, j, 0, x_peer),
+            remote(parts.at[4 * j + 1, upper], first.at[j, 1], sems, j, 1, x_peer),
+            remote(parts.at[4 * j, lower], first.at[j, 2], sems, j, 2, y_peer),
+            remote(parts.at[4 * j + 2, lower], first.at[j, 3], sems, j, 3, y_peer),
+        )
+
+    def late(j):
+        return (
+            remote(sums.at[j, 0], second.at[j, 0], sems, j, 4, y_peer),
+            remote(sums.at[j, 1], second.at[j, 1], sems, j, 5, x_peer),
+        )
+
+    def final(j):
+        return remote(ended.at[j], landing.at[j], sems, j, 6, target)
+
+    def compute(j):
+        for q in range(4):
+            t = 4 * j + q
+            load(t).wait()
+            value = tiles[t % buffers]
+            high = value.astype(jnp.bfloat16)
+            low = (value - high.astype(jnp.float32)).astype(jnp.bfloat16)
+            both = dot(turned[...], jnp.concatenate([high, low], axis=1))
+            parts[t] = both[:, :LANES] + both[:, LANES:]
+            if t + buffers < 4 * pieces:
+                load(t + buffers).start()
+            copies = early(j)
+            for i in ((0, 2), (1,), (3,), ())[q]:
+                copies[i].start()
+
+    def forward(j):
+        copies = early(j)
+        copies[0].wait_recv()
+        sums[j, 0] = parts[4 * j + 2, upper] + first[j, 0]
+        late(j)[0].start()
+        copies[2].wait_recv()
+        sums[j, 1] = parts[4 * j + 1, lower] + first[j, 2]
+        late(j)[1].start()
+
+    def end(j):
+        copies = early(j)
+        copies[1].wait_recv()
+        copies[3].wait_recv()
+        late(j)[0].wait_recv()
+        late(j)[1].wait_recv()
+        ended[j, upper] = parts[4 * j + 3, upper] + first[j, 1] + second[j, 0]
+        ended[j, lower] = parts[4 * j + 3, lower] + first[j, 3] + second[j, 1]
+
+        @pl.when(place != here)
+        def _():
+            final(j).start()
+
+    for j in range(pieces):
+        compute(j)
+        if j >= 1:
+            forward(j - 1)
+        if j >= 2:
+            end(j - 2)
+    forward(pieces - 1)
+    for j in range(max(pieces - 2, 0), pieces):
+        end(j)
+    for j in range(pieces):
+        lanes = pl.ds(j * LANES, LANES)
+
+        @pl.when(place != here)
+        def _():
+            final(j).wait_recv()
+            out[:, lanes] = landing[j]
+            final(j).wait_send()
+
+        @pl.when(place == here)
+        def _():
+            out[:, lanes] = ended[j]
+
+        for copy in early(j) + late(j):
+            copy.wait_send()
+
+
+def product(turned, ancestor):
+    height, depth = turned.shape
+    slab = ancestor.shape[1] // lax.axis_size("prow")
+    pieces = slab // LANES
+    half = height // 2
+    vmem = pl.BlockSpec(memory_space=pltpu.VMEM)
+    f32 = jnp.float32
+    return pl.pallas_call(
+        product_kernel,
+        out_shape=jax.ShapeDtypeStruct((height, slab), f32),
+        in_specs=[vmem, pl.BlockSpec(memory_space=pl.ANY)],
+        out_specs=vmem,
+        scratch_shapes=[
+            pltpu.VMEM((4, depth, LANES), f32),
+            pltpu.VMEM((4 * pieces, height, LANES), f32),
+            pltpu.VMEM((pieces, 4, half, LANES), f32),
+            pltpu.VMEM((pieces, 2, half, LANES), f32),
+            pltpu.VMEM((pieces, 2, half, LANES), f32),
+            pltpu.VMEM((pieces, height, LANES), f32),
+            pltpu.VMEM((pieces, height, LANES), f32),
+            pltpu.SemaphoreType.DMA((4 * pieces,)),
+            pltpu.SemaphoreType.DMA((2, pieces, 7)),
+        ],
+        compiler_params=pltpu.CompilerParams(
+            collective_id=1, has_side_effects=True, vmem_limit_bytes=48 * 1024 * 1024
+        ),
+    )(turned, ancestor)
+
+
+def product_plain(turned, ancestor):
+    n_rows = lax.axis_size("prow")
+    n_cols = lax.axis_size("pcol")
+    high, low = split(ancestor)
+    partial = dot(turned, high) + dot(turned, low)
+    summed = lax.psum_scatter(partial, "prow", scatter_dimension=1, tiled=True)
+    pairs = [(r * n_cols + c, c * n_rows + r) for r in range(n_rows) for c in range(n_cols)]
+    return lax.ppermute(summed, ("prow", "pcol"), pairs)
+
+
 def shards(ancestor, factor, inverse_diag, block_mask):
     rows_here = ancestor.shape[0]
     count, _, width = factor.shape
@@ -137,11 +310,8 @@
     own_mask = lax.dynamic_slice_in_dim(row_mask, grid_row * rows_here, rows_here, 1)
     masked = factor * own_mask[:, :, None].astype(factor.dtype)
     turned = masked.transpose(0, 2, 1).reshape(count * width, rows_here)
-    high, low = split(ancestor)
-    partial = dot(turned, high) + dot(turned, low)
-    summed = lax.psum_scatter(partial, "prow", scatter_dimension=1, tiled=True)
-    pairs = [(r * n_cols + c, c * n_rows + r) for r in range(n_rows) for c in range(n_cols)]
-    placed = lax.ppermute(summed, ("prow", "pcol"), pairs)
+    fits = n_rows == 4 and count % 2 == 0 and slab % LANES == 0
+    placed = (product if fits else product_plain)(turned, ancestor)
     slab_mask = lax.dynamic_slice_in_dim(own_mask, column * slab, slab, 1)
     placed = placed.reshape(count, width, slab)
     column_block = -slab_mask[:, :, None] * placed.transpose(0, 2, 1)

time: 151 us -> 108 us (0.72)
  waiting for transfers between devices: 46.8 us -> 0 us
  Pallas kernels: 53.9 us -> 85.9 us
  matrix products: 26.3 us -> 3.02 us
  between operations: 14.2 us -> 0.78 us
  other arithmetic: 2.02 us -> 7.45 us
  local copies, waits for them, and re-layouts: 5.51 us -> 10.8 us
  starting transfers between devices: 1.82 us -> 0 us
    pallas_call x0 -> x1, Pallas kernels: none -> 50.2 us  [product(): pl.pallas_call(product_kernel, out_shape=jax.ShapeDtypeStruct((height, sl...]
    reduce_scatter x1 -> x0, waiting for transfers between devices: 46.8 us -> none  [shards(): summed = lax.psum_scatter(partial, 'prow', scatter_dimension=1, tiled=True)]
    dot_general x6 -> x4, matrix products: 26.3 us -> 3.02 us  [dot(): return jnp.dot(a, b, preferred_element_type=jnp.float32)]
    pallas_call x1, Pallas kernels: 53.9 us -> 35.6 us  [finish(): pl.pallas_call(diagonal_kernel, out_shape=jax.ShapeDtypeStruct((height, w...]
    transpose x0 -> x1, other arithmetic: none -> 3.54 us  [shards(): turned = masked.transpose(0, 2, 1).reshape(count * width, rows_here)]
    transpose x0 -> x1, local copies, waits for them, and re-layouts: none -> 3.18 us  [shards(): turned = masked.transpose(0, 2, 1).reshape(count * width, rows_here)]
    reshape x1, local copies, waits for them, and re-layouts: 0.26 us -> 2.45 us  [shards(): placed = placed.reshape(count, width, slab)]
    ppermute x1 -> x0, starting transfers between devices: 1.78 us -> none  [shards(): placed = lax.ppermute(summed, ('prow', 'pcol'), pairs)]
  transfers between devices with their start and end apart: 2 -> 0, of which waited for: 1 -> 0; matrix products, arithmetic and copies ran while one was open for 0% -> 0% of each run, Pallas kernels for 0% -> 0%
where the time goes in v3:
time: 108 us
  Pallas kernels  85.9 us (80%)
  local copies, waits for them, and re-layouts  10.8 us (10%)
  other arithmetic  7.45 us (7%)
  matrix products  3.02 us (3%)
    pallas_call x1, Pallas kernels, product(): pl.pallas_call(product_kernel, out_shape=jax.ShapeDtypeStruct((height, sl...  50.2 us
    pallas_call x1, Pallas kernels, finish(): pl.pallas_call(diagonal_kernel, out_shape=jax.ShapeDtypeStruct((height, w...  35.6 us
    unnamed x13, local copies, waits for them, and re-layouts  5.16 us
    transpose x1, other arithmetic, shards(): turned = masked.transpose(0, 2, 1).reshape(count * width, rows_here)  3.54 us
    transpose x1, local copies, waits for them, and re-layouts, shards(): turned = masked.transpose(0, 2, 1).reshape(count * width, rows_here)  3.18 us
    dot_general x4, matrix products, dot(): return jnp.dot(a, b, preferred_element_type=jnp.float32)  3.02 us
    reshape x1, local copies, waits for them, and re-layouts, shards(): placed = placed.reshape(count, width, slab)  2.45 us

profile of v3, /device:TPU:0, one launch (start us, length us, event | category | flops | bytes accessed | tf_op | source)
XLA Modules:
  0.0 107.9 jit_solution(15527568806301676790)
XLA Ops:
  0.6 0.7 convert_element_type.17
  1.3 0.1 broadcast_bitcast_fusion
  1.4 0.1 copy.8
  1.5 0.1 dynamic-slice_negate_fusion
  1.6 3.5 %fusion.9 = bf16[2,256,3072]{1,2,0:T(8,128)(2,1)} fusion(bf16[2,3072,256]{2,1,0:T(8,128)(2,1)} %param.5, bf16[2,3072]{1,0:T(2,128)(2,1)S(1)} %dynamic-slice_convert_fusion), kind=kLoop, calls=%fused_computation.25 | loop fusion | flops 1572864 | bytes 6303744 | tf_op jit(solution)/shard_map/transpose | solution.py:312
  5.1 3.2 %copy.6 = bf16[2,256,3072]{2,1,0:T(8,128)(2,1)S(1)} copy(bf16[2,256,3072]{1,2,0:T(8,128)(2,1)} %fusion.9) | data formatting | bytes 6291456 | tf_op jit(solution)/shard_map/transpose | solution.py:312
  8.3 50.2 %shard_map.59 = f32[512,384]{1,0:T(8,128)S(1)} custom-call(bf16[512,3072]{1,0:T(8,128)(2,1)S(1)} %bitcast.37, f32[3072,1536]{1,0:T(8,128)} %ancestor.1), custom_call_target="tpu_custom_call" | custom-call | tf_op jit(solution)/shard_map/pallas_call | solution.py:269
  58.6 0.0 copy-start
  58.6 0.9 copy-done
  59.4 2.4 %copy.7 = f32[2,256,384]{1,2,0:T(8,128)} copy(f32[2,256,384]{2,1,0:T(8,128)} %bitcast.38) | data formatting | bytes 1572864 | tf_op jit(solution)/shard_map/reshape | solution.py:316
  61.9 1.3 %fusion.2 = (bf16[2,384,256]{2,1,0:T(8,128)(2,1)S(1)}, f32[2,384,256]{2,1,0:T(8,128)S(1)}) fusion(f32[2,256,384]{1,2,0:T(8,128)} %copy.7, f32[2,384]{1,0:T(2,128)S(1)} %dynamic-slice_negate_fusion), kind=kLoop, calls=%fused_computation.7 | loop fusion | flops 786432 | bytes 1969152 | tf_op jit(solution)/shard_map/convert_element_type | solution.py:14
  63.2 0.0 copy-start.3
  63.2 0.9 copy-done.3
  64.1 0.0 copy-done.1
  64.1 0.0 copy-start.4
  64.1 1.0 broadcast_multiply_fusion
  65.2 0.3 fusion.4
  65.4 1.4 %copy-done.2 = bf16[2,3072,256]{2,1,0:T(8,128)(2,1)} copy-done((bf16[2,3072,256]{2,1,0:T(8,128)(2,1)}, bf16[2,3072,256]{2,1,0:T(8,128)(2,1)S(1)}, u32[]{:S(2)}) %copy-start.2) | copy-done | bytes 3145752
  66.8 0.3 fusion.1
  67.1 1.3 %fusion.3 = f32[256,256]{1,0:T(8,128)S(1)} fusion(bf16[2,384,256]{2,1,0:T(8,128)(2,1)} %copy-done.4, bf16[2,3072,256]{2,1,0:T(8,128)(2,1)} %copy-done.2, s32[]{:T(128)S(6)} %add.19, s32[]{:T(128)S(6)} %select_n.11), kind=kOutput, calls=%fused_computation.12 | convolution fusion | flops 50331648 | bytes 655368 | tf_op jit(solution)/shard_map/dot_general | solution.py:18
  68.4 1.2 %fusion = f32[1,256,256]{2,1,0:T(8,128)S(1)} fusion(f32[256,256]{1,0:T(8,128)S(1)} %fusion.3, bf16[2,384,256]{2,1,0:T(8,128)(2,1)S(1)} %get-tuple-element.2, bf16[2,3072,256]{2,1,0:T(8,128)(2,1)} %copy-done.2, s32[]{:T(128)S(6)} %add.19, s32[]{:T(128)S(6)} %select_n.11), kind=kOutput, calls=%fused_computation.2 | convolution fusion | flops 50397184 | bytes 917512 | tf_op jit(solution)/shard_map/dot_general | solution.py:18
  69.6 0.8 pad_maximum_fusion
  70.4 35.6 %shard_map.60 = f32[512,256]{1,0:T(8,128)} custom-call(f32[512,256]{1,0:T(8,128)} %bitcast.39, bf16[512,256]{1,0:T(8,128)(2,1)} %bitcast.41), custom_call_target="tpu_custom_call" | custom-call | tf_op jit(solution)/shard_map/pallas_call | solution.py:118
  106.0 1.9 %copy.10 = f32[2,256,256]{2,1,0:T(8,128)} copy(f32[2,256,256]{2,1,0:T(8,128)} %bitcast.40) | data formatting | bytes 1048576
  (5 shorter events, 0.1 us)
Async XLA Ops:
  58.6 0.9 copy-start
  59.4 4.7 %copy-start.1 = (bf16[2,3072,256]{2,1,0:T(8,128)(2,1)S(1)}, bf16[2,3072,256]{2,1,0:T(8,128)(2,1)}, u32[]{:S(2)}) copy-start(bf16[2,3072,256]{2,1,0:T(8,128)(2,1)} %param.5) | copy-start | bytes 9437188
  63.2 0.9 copy-start.3
  64.1 1.0 copy-start.4
  65.1 1.7 %copy-start.2 = (bf16[2,3072,256]{2,1,0:T(8,128)(2,1)}, bf16[2,3072,256]{2,1,0:T(8,128)(2,1)S(1)}, u32[]{:S(2)}) copy-start(bf16[2,3072,256]{2,1,0:T(8,128)(2,1)S(1)} %broadcast_multiply_fusion) | copy-start | bytes 9437188

commit v4 on v3

--- a/solution.py
+++ b/solution.py
@@ -34,18 +34,11 @@
     )
 
 
-def greet(peers):
-    barrier = pltpu.get_barrier_semaphore()
-    for peer in peers:
-        pl.semaphore_signal(barrier, inc=1, device_id=peer, device_id_type=MESH)
-    pl.semaphore_wait(barrier, len(peers))
-
-
 def part(ref, start, size):
     return ref.at[pl.ds(pl.multiple_of(start, 8), size)]
 
 
-def sum_everywhere(term, acc, landed, gathered, sems):
+def sum_everywhere(term, acc, landed, gathered, sems, meanwhile):
     height = term.shape[0]
     start = 0
     size = height
@@ -54,7 +47,7 @@
     starts = []
     number = 0
     slot = 0
-    for n, mine, device in levels():
+    for depth, (n, mine, device) in enumerate(levels()):
         size = size // n
         copies = []
         for d in range(1, n):
@@ -70,6 +63,8 @@
             copy.start()
             copies.append(copy)
             number += 1
+        if depth == 1:
+            meanwhile()
         start = start + mine * size
         starts.append((start, size))
         total = part(source, start, size)[...]
@@ -103,28 +98,6 @@
         copy.wait_send()
 
 
-def diagonal_kernel(term, inverse, out, acc, landed, gathered, sems):
-    greet([device(lax.rem(mine + d, n)) for n, mine, device in levels() for d in range(1, n)])
-    sum_everywhere(term, acc, landed, gathered, sems)
-    out[...] = inverse[...].astype(jnp.float32) - gathered[...]
-
-
-def finish(term, inverse):
-    height, width = term.shape
-    sizes = [2, lax.axis_size("prow"), lax.axis_size("pcol") // 2]
-    copies = sum(n - 1 for n in sizes) * 2
-    block = pltpu.VMEM((height, width), jnp.float32)
-    vmem = pl.BlockSpec(memory_space=pltpu.VMEM)
-    return pl.pallas_call(
-        diagonal_kernel,
-        out_shape=jax.ShapeDtypeStruct((height, width), jnp.float32),
-        in_specs=[vmem, vmem],
-        out_specs=vmem,
-        scratch_shapes=[block, block, block, pltpu.SemaphoreType.DMA((2, copies))],
-        compiler_params=pltpu.CompilerParams(collective_id=0, has_side_effects=True),
-    )(term, inverse)
-
-
 LANES = 128
 
 
@@ -139,14 +112,36 @@
     )
 
 
-def product_kernel(turned, ancestor, out, tiles, parts, first, second, sums, ended, landing, loads, sems):
+def fused_kernel(
+    factor,
+    mask,
+    ancestor,
+    out,
+    gathered,
+    turned,
+    tiles,
+    parts,
+    first,
+    second,
+    sums,
+    ended,
+    landing,
+    term,
+    acc,
+    landed,
+    result,
+    loads,
+    sems,
+    small_sems,
+):
     n_rows = lax.axis_size("prow")
     n_cols = lax.axis_size("pcol")
     row = lax.axis_index("prow")
     column = lax.axis_index("pcol")
+    count, rows_here, width = factor.shape
     slab = out.shape[1]
     pieces = slab // LANES
-    half = out.shape[0] // 2
+    half = count * width // 2
     flip_x = row + 1 - 2 * lax.rem(row, 2)
     flip_y = lax.rem(row + 2, 4)
     flip_both = 3 - row
@@ -167,17 +162,26 @@
         load(t).start()
 
     barrier = pltpu.get_barrier_semaphore()
-    pl.semaphore_signal(barrier, inc=1, device_id=x_peer, device_id_type=MESH)
-    pl.semaphore_signal(barrier, inc=1, device_id=y_peer, device_id_type=MESH)
+    peers = [device(lax.rem(mine + d, n)) for n, mine, device in levels() for d in range(1, n)]
+    for peer in peers:
+        pl.semaphore_signal(barrier, inc=1, device_id=peer, device_id_type=MESH)
 
     @pl.when(place != here)
     def _():
         pl.semaphore_signal(barrier, inc=1, device_id=origin, device_id_type=MESH)
-        pl.semaphore_wait(barrier, 3)
+
+    for k in range(count):
+        for i in range(0, rows_here, WIDTH):
+            block = factor[k, pl.ds(i, WIDTH)].T.astype(jnp.float32) * mask[pl.ds(k, 1), pl.ds(i, WIDTH)]
+            turned[pl.ds(k * width, width), pl.ds(i, WIDTH)] = block.astype(jnp.bfloat16)
+
+    @pl.when(place != here)
+    def _():
+        pl.semaphore_wait(barrier, len(peers) + 1)
 
     @pl.when(place == here)
     def _():
-        pl.semaphore_wait(barrier, 2)
+        pl.semaphore_wait(barrier, len(peers))
 
     def early(j):
         return (
@@ -233,6 +237,10 @@
         def _():
             final(j).start()
 
+        @pl.when(place == here)
+        def _():
+            landing[j] = ended[j]
+
     for j in range(pieces):
         compute(j)
         if j >= 1:
@@ -242,36 +250,65 @@
     forward(pieces - 1)
     for j in range(max(pieces - 2, 0), pieces):
         end(j)
+    totals = [0.0] * count
     for j in range(pieces):
-        lanes = pl.ds(j * LANES, LANES)
-
         @pl.when(place != here)
         def _():
             final(j).wait_recv()
-            out[:, lanes] = landing[j]
+
+        lanes = pl.ds(pl.multiple_of(column * slab + j * LANES, LANES), LANES)
+        for k in range(count):
+            rows = pl.ds(k * width, width)
+            value = landing[j, rows]
+            high = value.astype(jnp.bfloat16)
+            low = (value - high.astype(jnp.float32)).astype(jnp.bfloat16)
+            own = turned[rows, lanes]
+            totals[k] = totals[k] + lax.dot_general(
+                jnp.concatenate([own, own], axis=1),
+                jnp.concatenate([high, low], axis=1),
+                (((1,), (1,)), ((), ())),
+                preferred_element_type=jnp.float32,
+            )
+    for k in range(count):
+        term[pl.ds(k * width, width)] = totals[k]
+
+    def meanwhile():
+        for j in range(pieces):
+            for k in range(count):
+                out[k, pl.ds(j * LANES, LANES)] = landing[j, pl.ds(k * width, width)].T
+
+    sum_everywhere(term, acc, landed, result, small_sems, meanwhile)
+    gathered[...] = result[...]
+    for j in range(pieces):
+        @pl.when(place != here)
+        def _():
             final(j).wait_send()
-
-        @pl.when(place == here)
-        def _():
-            out[:, lanes] = ended[j]
 
         for copy in early(j) + late(j):
             copy.wait_send()
 
 
-def product(turned, ancestor):
-    height, depth = turned.shape
-    slab = ancestor.shape[1] // lax.axis_size("prow")
+def fused(factor, mask, ancestor):
+    count, depth, width = factor.shape
+    height = count * width
+    n_rows, n_cols = lax.axis_size("prow"), lax.axis_size("pcol")
+    slab = ancestor.shape[1] // n_rows
     pieces = slab // LANES
     half = height // 2
     vmem = pl.BlockSpec(memory_space=pltpu.VMEM)
     f32 = jnp.float32
+    block = pltpu.VMEM((height, width), f32)
+    small = 2 * (1 + n_rows - 1 + n_cols // 2 - 1)
     return pl.pallas_call(
-        product_kernel,
-        out_shape=jax.ShapeDtypeStruct((height, slab), f32),
-        in_specs=[vmem, pl.BlockSpec(memory_space=pl.ANY)],
-        out_specs=vmem,
+        fused_kernel,
+        out_shape=(
+            jax.ShapeDtypeStruct((count, slab, width), f32),
+            jax.ShapeDtypeStruct((height, width), f32),
+        ),
+        in_specs=[vmem, vmem, pl.BlockSpec(memory_space=pl.ANY)],
+        out_specs=(vmem, vmem),
         scratch_shapes=[
+            pltpu.VMEM((height, depth), jnp.bfloat16),
             pltpu.VMEM((4, depth, LANES), f32),
             pltpu.VMEM((4 * pieces, height, LANES), f32),
             pltpu.VMEM((pieces, 4, half, LANES), f32),
@@ -279,13 +316,18 @@
             pltpu.VMEM((pieces, 2, half, LANES), f32),
             pltpu.VMEM((pieces, height, LANES), f32),
             pltpu.VMEM((pieces, height, LANES), f32),
+            block,
+            block,
+            block,
+            block,
             pltpu.SemaphoreType.DMA((4 * pieces,)),
             pltpu.SemaphoreType.DMA((2, pieces, 7)),
+            pltpu.SemaphoreType.DMA((2, small)),
         ],
         compiler_params=pltpu.CompilerParams(
             collective_id=1, has_side_effects=True, vmem_limit_bytes=48 * 1024 * 1024
         ),
-    )(turned, ancestor)
+    )(factor, mask, ancestor)
 
 
 def product_plain(turned, ancestor):
@@ -308,23 +350,21 @@
     slab = rows_here // n_cols
     row_mask = jnp.repeat(block_mask, WIDTH, axis=1).astype(jnp.float32)
     own_mask = lax.dynamic_slice_in_dim(row_mask, grid_row * rows_here, rows_here, 1)
+    slab_mask = lax.dynamic_slice_in_dim(own_mask, column * slab, slab, 1)
+    inverse = inverse_diag.astype(jnp.float32)
+    fits = n_rows == 4 and n_cols % 2 == 0 and count % 2 == 0
+    fits = fits and slab % LANES == 0 and count * width % (8 * n_rows * n_cols) == 0
+    if fits:
+        placed, total = fused(factor, own_mask, ancestor)
+        return (-slab_mask[:, :, None] * placed, inverse + total.reshape(inverse.shape))
     masked = factor * own_mask[:, :, None].astype(factor.dtype)
     turned = masked.transpose(0, 2, 1).reshape(count * width, rows_here)
-    fits = n_rows == 4 and count % 2 == 0 and slab % LANES == 0
-    placed = (product if fits else product_plain)(turned, ancestor)
-    slab_mask = lax.dynamic_slice_in_dim(own_mask, column * slab, slab, 1)
-    placed = placed.reshape(count, width, slab)
+    placed = product_plain(turned, ancestor).reshape(count, width, slab)
     column_block = -slab_mask[:, :, None] * placed.transpose(0, 2, 1)
     own_slab = lax.dynamic_slice_in_dim(masked, column * slab, slab, 1)
     high, low = split(column_block)
     term = jnp.stack([dot(own_slab[k].T, high[k]) + dot(own_slab[k].T, low[k]) for k in range(count)])
-    devices = n_rows * n_cols
-    if n_cols % 2 or (count * width) % (8 * devices):
-        total = lax.psum(term, ("prow", "pcol"))
-        return (column_block, inverse_diag.astype(jnp.float32) - total)
-    flat = (count * width, width)
-    diagonal = finish(term.reshape(flat), inverse_diag.reshape(flat))
-    return (column_block, diagonal.reshape(inverse_diag.shape))
+    return (column_block, inverse - lax.psum(term, ("prow", "pcol")))
 
 
 def solution(mesh):

time: 108 us -> 86.1 us (0.80)
  local copies, waits for them, and re-layouts: 10.8 us -> 2.05 us
  Pallas kernels: 85.9 us -> 80.5 us
  other arithmetic: 7.45 us -> 2.71 us
  matrix products: 3.02 us -> 0 us
    pallas_call x2 -> x1, Pallas kernels: 85.9 us -> 80.5 us  [fused(): pl.pallas_call(fused_kernel, out_shape=(jax.ShapeDtypeStruct((count, slab...]
    transpose x1 -> x0, other arithmetic: 3.54 us -> none  [shards(): turned = masked.transpose(0, 2, 1).reshape(count * width, rows_here)]
    transpose x1 -> x0, local copies, waits for them, and re-layouts: 3.18 us -> none  [shards(): turned = masked.transpose(0, 2, 1).reshape(count * width, rows_here)]
    unnamed x13 -> x6, local copies, waits for them, and re-layouts: 5.16 us -> 2.05 us
    dot_general x4 -> x0, matrix products: 3.02 us -> none  [dot(): return jnp.dot(a, b, preferred_element_type=jnp.float32)]
    reshape x1 -> x0, local copies, waits for them, and re-layouts: 2.45 us -> none  [shards(): placed = placed.reshape(count, width, slab)]
    convert_element_type x2 -> x0, other arithmetic: 1.34 us -> none  [split(): return (high.astype(jnp.bfloat16), low.astype(jnp.bfloat16))]
where the time goes in v4:
time: 86.1 us; the launch traced here: 85.9 us
  Pallas kernels  80.5 us (93%)
  other arithmetic  2.71 us (3%)
  local copies, waits for them, and re-layouts  2.05 us (2%)
    pallas_call x1, Pallas kernels, fused(): pl.pallas_call(fused_kernel, out_shape=(jax.ShapeDtypeStruct((count, slab...  80.5 us
    unnamed x6, local copies, waits for them, and re-layouts  2.05 us

profile of v4, /device:TPU:0, one launch (start us, length us, event | category | flops | bytes accessed | tf_op | source)
XLA Modules:
  0.0 85.9 jit_solution(2759346286783338678)
XLA Ops:
  0.6 0.0 copy-start.1
  0.7 0.7 convert_element_type.10
  1.4 0.1 broadcast_bitcast_fusion
  1.5 0.1 copy.6
  1.5 0.1 dynamic-slice_negate_fusion
  1.6 0.0 copy-start
  1.6 1.9 %copy-done = bf16[2,3072,256]{2,1,0:T(8,128)(2,1)S(1)} copy-done((bf16[2,3072,256]{2,1,0:T(8,128)(2,1)S(1)}, bf16[2,3072,256]{2,1,0:T(8,128)(2,1)}, u32[]{:S(2)}) %copy-start) | copy-done | bytes 3145752
  3.5 80.5 %shard_map.59 = (f32[2,384,256]{2,1,0:T(8,128)S(1)}, f32[512,256]{1,0:T(8,128)S(1)}) custom-call(bf16[2,3072,256]{2,1,0:T(8,128)(2,1)S(1)} %copy-done, f32[2,3072]{1,0:T(2,128)S(1)} %constant_dynamic-slice_fusion.mask, f32[3072,1536]{1,0:T(8,128)} %ancestor.1), custom_call_target="tpu_custom_call" | custom-call | tf_op jit(solution)/shard_map/pallas_call | solution.py:302
  84.0 1.0 %broadcast_multiply_fusion = f32[2,384,256]{2,1,0:T(8,128)} fusion(f32[2,384,256]{2,1,0:T(8,128)S(1)} %get-tuple-element.4, f32[2,384]{1,0:T(2,128)S(1)} %dynamic-slice_negate_fusion), kind=kLoop, calls=%fused_computation.1 | loop fusion | flops 196608 | bytes 1575936 | tf_op jit(solution)/shard_map/mul | solution.py:359
  85.1 0.0 copy-done.1
  85.1 0.9 %convert_add_fusion = f32[2,256,256]{2,1,0:T(8,128)} fusion(f32[2,256,256]{2,1,0:T(8,128)S(1)} %bitcast.4, bf16[2,256,256]{2,1,0:T(8,128)(2,1)S(1)} %copy-done.1), kind=kLoop, calls=%fused_computation | loop fusion | flops 262144 | bytes 1310720 | tf_op jit(solution)/shard_map/add | solution.py:359
  (1 shorter events, 0.0 us)
Async XLA Ops:
  0.6 84.4 %copy-start.1 = (bf16[2,256,256]{2,1,0:T(8,128)(2,1)S(1)}, bf16[2,256,256]{2,1,0:T(8,128)(2,1)}, u32[]{:S(2)}) copy-start(bf16[2,256,256]{2,1,0:T(8,128)(2,1)} %param.6) | copy-start | bytes 786436
  1.6 1.9 %copy-start = (bf16[2,3072,256]{2,1,0:T(8,128)(2,1)S(1)}, bf16[2,3072,256]{2,1,0:T(8,128)(2,1)}, u32[]{:S(2)}) copy-start(bf16[2,3072,256]{2,1,0:T(8,128)(2,1)} %factor.1) | copy-start | bytes 9437188

commit v5 on v4

--- a/solution.py
+++ b/solution.py
@@ -38,16 +38,14 @@
     return ref.at[pl.ds(pl.multiple_of(start, 8), size)]
 
 
-def sum_everywhere(term, acc, landed, gathered, sems, meanwhile):
-    height = term.shape[0]
-    start = 0
+def sum_everywhere(term, acc, landed, gathered, sems, base, height, number):
+    start = base
     size = height
+    slot = base
     source = term
     sent = []
     starts = []
-    number = 0
-    slot = 0
-    for depth, (n, mine, device) in enumerate(levels()):
+    for n, mine, device in levels():
         size = size // n
         copies = []
         for d in range(1, n):
@@ -63,8 +61,7 @@
             copy.start()
             copies.append(copy)
             number += 1
-        if depth == 1:
-            meanwhile()
+        yield
         start = start + mine * size
         starts.append((start, size))
         total = part(source, start, size)[...]
@@ -91,11 +88,24 @@
             copy.start()
             copies.append(copy)
             number += 1
+        yield
         for copy in copies:
             copy.wait_recv()
         sent += copies
     for copy in sent:
         copy.wait_send()
+
+
+def chunk_of(position, deep):
+    across = lax.rem(position + deep, 2)
+    along = lax.rem(lax.div(position, 2) + lax.div(deep, 2), 2)
+    return 2 * lax.rem(across + along, 2) + along
+
+
+def position_of(chunk, deep):
+    along = lax.rem(chunk, 2)
+    across = lax.rem(lax.div(chunk, 2) + along, 2)
+    return lax.rem(across + deep, 2) + 2 * lax.rem(along + lax.div(deep, 2), 2)
 
 
 LANES = 128
@@ -146,16 +156,18 @@
     flip_y = lax.rem(row + 2, 4)
     flip_both = 3 - row
     x_peer, y_peer = (flip_x, column), (flip_y, column)
-    place = column * n_rows + row
+    deep = lax.div(column, 2)
+    place = column * n_rows + chunk_of(row, deep)
     target = (lax.div(place, n_cols), lax.rem(place, n_cols))
     here = row * n_cols + column
-    origin = (lax.rem(here, n_rows), lax.div(here, n_rows))
+    from_column = lax.div(here, n_rows)
+    origin = (position_of(lax.rem(here, n_rows), lax.div(from_column, 2)), from_column)
     order = (flip_both, flip_x, flip_y, row)
     buffers = tiles.shape[0]
     upper, lower = pl.ds(0, half), pl.ds(half, half)
 
     def load(t):
-        start = pl.multiple_of(order[t % 4] * slab + (t // 4) * LANES, LANES)
+        start = pl.multiple_of(chunk_of(order[t % 4], deep) * slab + (t // 4) * LANES, LANES)
         return pltpu.make_async_copy(ancestor.at[:, pl.ds(start, LANES)], tiles.at[t % buffers], loads.at[t])
 
     for t in range(buffers):
@@ -277,7 +289,15 @@
             for k in range(count):
                 out[k, pl.ds(j * LANES, LANES)] = landing[j, pl.ds(k * width, width)].T
 
-    sum_everywhere(term, acc, landed, result, small_sems, meanwhile)
+    each = small_sems.shape[1] // 2
+    halves = [
+        sum_everywhere(term, acc, landed, result, small_sems, h * half, half, h * each) for h in range(2)
+    ]
+    for depth in range(7):
+        for running in halves:
+            next(running, None)
+        if depth == 1:
+            meanwhile()
     gathered[...] = result[...]
     for j in range(pieces):
         @pl.when(place != here)
@@ -298,7 +318,7 @@
     vmem = pl.BlockSpec(memory_space=pltpu.VMEM)
     f32 = jnp.float32
     block = pltpu.VMEM((height, width), f32)
-    small = 2 * (1 + n_rows - 1 + n_cols // 2 - 1)
+    small = 4 * (1 + n_rows - 1 + n_cols // 2 - 1)
     return pl.pallas_call(
         fused_kernel,
         out_shape=(
@@ -353,7 +373,7 @@
     slab_mask = lax.dynamic_slice_in_dim(own_mask, column * slab, slab, 1)
     inverse = inverse_diag.astype(jnp.float32)
     fits = n_rows == 4 and n_cols % 2 == 0 and count % 2 == 0
-    fits = fits and slab % LANES == 0 and count * width % (8 * n_rows * n_cols) == 0
+    fits = fits and slab % LANES == 0 and count * width % (16 * n_rows * n_cols) == 0
     if fits:
         placed, total = fused(factor, own_mask, ancestor)
         return (-slab_mask[:, :, None] * placed, inverse + total.reshape(inverse.shape))

time: 86.1 us -> 76.9 us (0.89)
  Pallas kernels: 80.5 us -> 71.3 us
    pallas_call x1, Pallas kernels: 80.5 us -> 71.3 us  [fused(): pl.pallas_call(fused_kernel, out_shape=(jax.ShapeDtypeStruct((count, slab...]
where the time goes in v5:
time: 76.9 us; the launch traced here: 76.7 us
  Pallas kernels  71.3 us (93%)
  other arithmetic  2.71 us (4%)
  local copies, waits for them, and re-layouts  2.05 us (3%)
    pallas_call x1, Pallas kernels, fused(): pl.pallas_call(fused_kernel, out_shape=(jax.ShapeDtypeStruct((count, slab...  71.3 us
    unnamed x6, local copies, waits for them, and re-layouts  2.05 us

profile of v5, /device:TPU:0, one launch (start us, length us, event | category | flops | bytes accessed | tf_op | source)
XLA Modules:
  0.0 76.7 jit_solution(16540097460078234389)
XLA Ops:
  0.6 0.0 copy-start.1
  0.7 0.7 convert_element_type.10
  1.4 0.1 broadcast_bitcast_fusion
  1.5 0.1 copy.6
  1.5 0.1 dynamic-slice_negate_fusion
  1.6 0.0 copy-start
  1.6 1.9 %copy-done = bf16[2,3072,256]{2,1,0:T(8,128)(2,1)S(1)} copy-done((bf16[2,3072,256]{2,1,0:T(8,128)(2,1)S(1)}, bf16[2,3072,256]{2,1,0:T(8,128)(2,1)}, u32[]{:S(2)}) %copy-start) | copy-done | bytes 3145752
  3.5 71.3 %shard_map.59 = (f32[2,384,256]{2,1,0:T(8,128)S(1)}, f32[512,256]{1,0:T(8,128)S(1)}) custom-call(bf16[2,3072,256]{2,1,0:T(8,128)(2,1)S(1)} %copy-done, f32[2,3072]{1,0:T(2,128)S(1)} %constant_dynamic-slice_fusion.mask, f32[3072,1536]{1,0:T(8,128)} %ancestor.1), custom_call_target="tpu_custom_call" | custom-call | tf_op jit(solution)/shard_map/pallas_call | solution.py:322
  74.8 1.0 %broadcast_multiply_fusion = f32[2,384,256]{2,1,0:T(8,128)} fusion(f32[2,384,256]{2,1,0:T(8,128)S(1)} %get-tuple-element.4, f32[2,384]{1,0:T(2,128)S(1)} %dynamic-slice_negate_fusion), kind=kLoop, calls=%fused_computation.1 | loop fusion | flops 196608 | bytes 1575936 | tf_op jit(solution)/shard_map/mul | solution.py:379
  75.8 0.0 copy-done.1
  75.8 0.9 %convert_add_fusion = f32[2,256,256]{2,1,0:T(8,128)} fusion(f32[2,256,256]{2,1,0:T(8,128)S(1)} %bitcast.4, bf16[2,256,256]{2,1,0:T(8,128)(2,1)S(1)} %copy-done.1), kind=kLoop, calls=%fused_computation | loop fusion | flops 262144 | bytes 1310720 | tf_op jit(solution)/shard_map/add | solution.py:379
  (1 shorter events, 0.0 us)
Async XLA Ops:
  0.6 75.2 %copy-start.1 = (bf16[2,256,256]{2,1,0:T(8,128)(2,1)S(1)}, bf16[2,256,256]{2,1,0:T(8,128)(2,1)}, u32[]{:S(2)}) copy-start(bf16[2,256,256]{2,1,0:T(8,128)(2,1)} %param.6) | copy-start | bytes 786436
  1.6 1.9 %copy-start = (bf16[2,3072,256]{2,1,0:T(8,128)(2,1)S(1)}, bf16[2,3072,256]{2,1,0:T(8,128)(2,1)}, u32[]{:S(2)}) copy-start(bf16[2,3072,256]{2,1,0:T(8,128)(2,1)} %factor.1) | copy-start | bytes 9437188

commit v6 on v5

--- a/solution.py
+++ b/solution.py
@@ -226,6 +226,8 @@
             copies = early(j)
             for i in ((0, 2), (1,), (3,), ())[q]:
                 copies[i].start()
+            if j >= 1 and q == 1:
+                forward(j - 1)
 
     def forward(j):
         copies = early(j)
@@ -256,12 +258,9 @@
     for j in range(pieces):
         compute(j)
         if j >= 1:
-            forward(j - 1)
-        if j >= 2:
-            end(j - 2)
+            end(j - 1)
     forward(pieces - 1)
-    for j in range(max(pieces - 2, 0), pieces):
-        end(j)
+    end(pieces - 1)
     totals = [0.0] * count
     for j in range(pieces):
         @pl.when(place != here)

time: 76.9 us -> 77.1 us (level)
  no operation moved by 1% of the time
where the time goes in v6:
time: 77.1 us; the launch traced here: 76.9 us
  Pallas kernels  71.5 us (93%)
  other arithmetic  2.71 us (4%)
  local copies, waits for them, and re-layouts  2.05 us (3%)
    pallas_call x1, Pallas kernels, fused(): pl.pallas_call(fused_kernel, out_shape=(jax.ShapeDtypeStruct((count, slab...  71.5 us
    unnamed x6, local copies, waits for them, and re-layouts  2.05 us

profile of v6, /device:TPU:0, one launch (start us, length us, event | category | flops | bytes accessed | tf_op | source)
XLA Modules:
  0.0 76.9 jit_solution(14108138810992143975)
XLA Ops:
  0.6 0.0 copy-start.1
  0.7 0.7 convert_element_type.10
  1.4 0.1 broadcast_bitcast_fusion
  1.5 0.1 copy.6
  1.5 0.1 dynamic-slice_negate_fusion
  1.6 0.0 copy-start
  1.6 1.9 %copy-done = bf16[2,3072,256]{2,1,0:T(8,128)(2,1)S(1)} copy-done((bf16[2,3072,256]{2,1,0:T(8,128)(2,1)S(1)}, bf16[2,3072,256]{2,1,0:T(8,128)(2,1)}, u32[]{:S(2)}) %copy-start) | copy-done | bytes 3145752
  3.5 71.5 %shard_map.59 = (f32[2,384,256]{2,1,0:T(8,128)S(1)}, f32[512,256]{1,0:T(8,128)S(1)}) custom-call(bf16[2,3072,256]{2,1,0:T(8,128)(2,1)S(1)} %copy-done, f32[2,3072]{1,0:T(2,128)S(1)} %constant_dynamic-slice_fusion.mask, f32[3072,1536]{1,0:T(8,128)} %ancestor.1), custom_call_target="tpu_custom_call" | custom-call | tf_op jit(solution)/shard_map/pallas_call | solution.py:321
  75.0 1.0 %broadcast_multiply_fusion = f32[2,384,256]{2,1,0:T(8,128)} fusion(f32[2,384,256]{2,1,0:T(8,128)S(1)} %get-tuple-element.4, f32[2,384]{1,0:T(2,128)S(1)} %dynamic-slice_negate_fusion), kind=kLoop, calls=%fused_computation.1 | loop fusion | flops 196608 | bytes 1575936 | tf_op jit(solution)/shard_map/mul | solution.py:378
  76.0 0.0 copy-done.1
  76.0 0.9 %convert_add_fusion = f32[2,256,256]{2,1,0:T(8,128)} fusion(f32[2,256,256]{2,1,0:T(8,128)S(1)} %bitcast.4, bf16[2,256,256]{2,1,0:T(8,128)(2,1)S(1)} %copy-done.1), kind=kLoop, calls=%fused_computation | loop fusion | flops 262144 | bytes 1310720 | tf_op jit(solution)/shard_map/add | solution.py:378
  (1 shorter events, 0.0 us)
Async XLA Ops:
  0.6 75.4 %copy-start.1 = (bf16[2,256,256]{2,1,0:T(8,128)(2,1)S(1)}, bf16[2,256,256]{2,1,0:T(8,128)(2,1)}, u32[]{:S(2)}) copy-start(bf16[2,256,256]{2,1,0:T(8,128)(2,1)} %param.6) | copy-start | bytes 786436
  1.6 1.9 %copy-start = (bf16[2,3072,256]{2,1,0:T(8,128)(2,1)S(1)}, bf16[2,3072,256]{2,1,0:T(8,128)(2,1)}, u32[]{:S(2)}) copy-start(bf16[2,3072,256]{2,1,0:T(8,128)(2,1)} %factor.1) | copy-start | bytes 9437188
